TPU v7x, 32 devices: a whole 2x2x4 slice. The times are simulated.
32 devices in a mesh: dp: 8 (over z, core), tensor: 4 (over y, x).
Axes of the slice: x: 2, y: 2, z: 4, core: 2. Of those that a mesh axis runs over, the one named last changes fastest.
Arguments:
- tokens: bfloat16 [18432, 2048], P(('dp', 'tensor')), may hold values from -6 to 6
- cotangent: bfloat16 [18432, 2048], P(('dp', 'tensor')), may hold values from -6 to 6
- ln_gain: float32 [2048], replicated, may hold values from 0.5 to 1.5
- ln_bias: float32 [2048], replicated, may hold values from -3 to 3
- w_qkv: bfloat16 [3, 2048, 2048], P(None, 'dp', 'tensor')
- b_qkv: float32 [3, 2048], P(None, 'tensor'), may hold values from -3 to 3
- w_out: bfloat16 [2048, 2048], P('tensor', 'dp'), may hold values from -0.5 to 0.5
- w_fc1: bfloat16 [2048, 8192], P('dp', 'tensor'), may hold values from -0.125 to 0.125
- b_fc1: float32 [8192], P('tensor'), may hold values from -3 to 3
- w_fc2: bfloat16 [8192, 2048], P('tensor', 'dp'), may hold values from -0.0625 to 0.0625
- resid_bias: float32 [2048], replicated, may hold values from -3 to 3
- parents: int32 [8, 18], P('dp'), may hold values from 0 to 9, as said below
Outputs:
- output_rows: bfloat16 [18432, 2048], P(('dp', 'tensor'))
- input_grad: float32 [18432, 2048], P(('dp', 'tensor'))
- grad_small: float32 [3, 2048], P(None, ('dp', 'tensor'))
- grad_w_qkv: float32 [3, 2048, 2048], P(None, 'dp', 'tensor')
- grad_b_qkv: float32 [3, 2048], P(None, 'tensor')
- grad_w_out: float32 [2048, 2048], P('tensor', 'dp')
- grad_w_fc1: float32 [2048, 8192], P('dp', 'tensor')
- grad_b_fc1: float32 [8192], P('tensor')
- grad_w_fc2: float32 [8192, 2048], P('tensor', 'dp')
- clipped_qk: bfloat16 [2, 2048, 2048], P(None, 'dp', 'tensor')
Inputs may be any that keep to these rules, and one draw needn't show every extreme that they name: `parents`: in each tree, segment 0 is its own parent and segment i < 6 has parent i - 1; the next 4 segments have parent 6 - 1; each of these is the parent of exactly 2 of the remaining segments.
All inputs are finite; a program needn't handle non-finite values.
Results may differ from a plain program's by a relative error of at most 0.014.
Values may be sent and summed in bfloat16 or wider, within the bound.
A program may use at most 384 MiB of HBM per device.

v0:
```python
import jax
import jax.numpy as jnp
from jax import lax
from jax.sharding import PartitionSpec as P

HDIM = 64
ROT = 32
SEG = 128
QBLK = 768
clip_tau = 10.0
norm_eps = 1e-05
rope_base = 10000.0


def tree_layout(parent_ids, seg_len):
    seg_count = parent_ids.shape[0]
    labels = jnp.arange(seg_count, dtype=jnp.int32)
    current = labels
    depth_seg = jnp.zeros((seg_count,), jnp.int32)
    ancestry = labels[:, None] == labels[None, :]
    for step_index in range(seg_count):
        depth_seg = depth_seg + (current != 0).astype(jnp.int32)
        current = jnp.sum(
            jnp.where(current[:, None] == labels[None, :], parent_ids[None, :], 0), axis=1
        )
        ancestry = ancestry | (current[:, None] == labels[None, :])
    positions = jnp.repeat(depth_seg, seg_len) * seg_len + jnp.tile(
        jnp.arange(seg_len, dtype=jnp.int32), seg_count
    )
    return (positions, ancestry)


def rotary_tables(positions):
    half_rot = ROT // 2
    inverse_freq = 1.0 / rope_base ** (jnp.arange(half_rot, dtype=jnp.float32) * (2.0 / ROT))
    angles = positions.astype(jnp.float32)[:, None] * inverse_freq[None, :]
    return (jnp.cos(angles), jnp.sin(angles))


def rotate(block_in, cos_rows, sin_rows):
    half_rot = ROT // 2
    first_half = block_in[..., :half_rot]
    second_half = block_in[..., half_rot:ROT]
    cos_heads = cos_rows[:, None, :]
    sin_heads = sin_rows[:, None, :]
    return jnp.concatenate(
        [
            first_half * cos_heads - second_half * sin_heads,
            second_half * cos_heads + first_half * sin_heads,
            block_in[..., ROT:],
        ],
        axis=-1,
    )


def unrotate(grad_in, cos_rows, sin_rows):
    half_rot = ROT // 2
    first_half = grad_in[..., :half_rot]
    second_half = grad_in[..., half_rot:ROT]
    cos_heads = cos_rows[:, None, :]
    sin_heads = sin_rows[:, None, :]
    return jnp.concatenate(
        [
            first_half * cos_heads + second_half * sin_heads,
            second_half * cos_heads - first_half * sin_heads,
            grad_in[..., ROT:],
        ],
        axis=-1,
    )


def block_mask(ancestry, row_start, row_count, total_rows, seg_len):
    row_ids = row_start + jnp.arange(row_count, dtype=jnp.int32)
    col_ids = jnp.arange(total_rows, dtype=jnp.int32)
    seg_rows = lax.dynamic_slice_in_dim(ancestry, row_start // seg_len, row_count // seg_len, 0)
    widened = jnp.repeat(jnp.repeat(seg_rows, seg_len, axis=0), seg_len, axis=1)
    same_seg = row_ids[:, None] // seg_len == col_ids[None, :] // seg_len
    return widened & (~same_seg | (col_ids[None, :] <= row_ids[:, None]))


def norm_rows(rows_in, gain_in, shift_in):
    row_mean = jnp.mean(rows_in, axis=-1, keepdims=True)
    centred = rows_in - row_mean
    inverse = lax.rsqrt(jnp.mean(centred * centred, axis=-1, keepdims=True) + norm_eps)
    return centred * inverse * gain_in + shift_in


def gelu_tanh(values_in):
    return jax.nn.gelu(values_in, approximate=True)


def body(
    tokens,
    cotangent,
    ln_gain,
    ln_bias,
    w_qkv,
    b_qkv,
    w_out,
    w_fc1,
    b_fc1,
    w_fc2,
    resid_bias,
    parents,
):
    local_rows = tokens.shape[0]
    total_rows = local_rows * lax.axis_size("tensor")
    own_start = lax.axis_index("tensor") * local_rows
    head_count = w_qkv.shape[2] // HDIM
    score_scale = HDIM ** (-0.5)
    positions, ancestry = tree_layout(parents[0], SEG)
    cos_rows, sin_rows = rotary_tables(positions)
    block_starts = jnp.arange(total_rows // QBLK, dtype=jnp.int32) * QBLK
    tokens_f = tokens.astype(jnp.float32)
    normed_local = norm_rows(tokens_f, ln_gain, ln_bias).astype(jnp.bfloat16)
    qkv_w, out_w, up_w, down_w = (
        lax.all_gather(w_qkv, "dp", axis=1, tiled=True),
        lax.all_gather(w_out, "dp", axis=1, tiled=True),
        lax.all_gather(w_fc1, "dp", axis=0, tiled=True),
        lax.all_gather(w_fc2, "dp", axis=1, tiled=True),
    )
    normed = lax.all_gather(normed_local, "tensor", axis=0, tiled=True)
    projected = (
        jnp.einsum("td,cdh->cth", normed, qkv_w, preferred_element_type=jnp.float32)
        + b_qkv[:, None, :]
    )
    heads_view = projected.reshape(3, total_rows, head_count, HDIM)
    queries = rotate(heads_view[0], cos_rows, sin_rows).astype(jnp.bfloat16)
    keys_rot = rotate(heads_view[1], cos_rows, sin_rows).astype(jnp.bfloat16)
    values_all = heads_view[2].astype(jnp.bfloat16)

    def attend_block(row_start):
        query_rows = lax.dynamic_slice_in_dim(queries, row_start, QBLK, 0)
        raw_scores = (
            jnp.einsum("qhe,khe->hqk", query_rows, keys_rot, preferred_element_type=jnp.float32)
            * score_scale
        )
        allowed = block_mask(ancestry, row_start, QBLK, total_rows, SEG)
        masked = jnp.where(allowed[None], raw_scores, -1e30)
        row_top = jnp.max(masked, axis=2)
        exponent = jnp.exp(masked - row_top[..., None])
        row_total = jnp.sum(exponent, axis=2)
        probs_low = (exponent / row_total[..., None]).astype(jnp.bfloat16)
        attended_rows = jnp.einsum(
            "hqk,khe->qhe", probs_low, values_all, preferred_element_type=jnp.float32
        ).astype(jnp.bfloat16)
        return (attended_rows, row_top + jnp.log(row_total), jnp.max(row_top, axis=1))

    attended, log_totals, block_tops = lax.map(attend_block, block_starts)
    attended = attended.reshape(total_rows, head_count * HDIM)
    hidden_pre = jnp.dot(normed, up_w, preferred_element_type=jnp.float32) + b_fc1
    activated = gelu_tanh(hidden_pre).astype(jnp.bfloat16)
    branch_whole = lax.psum(
        jnp.dot(attended, out_w, preferred_element_type=jnp.float32)
        + jnp.dot(activated, down_w, preferred_element_type=jnp.float32),
        "tensor",
    )
    branch_sum = lax.dynamic_slice_in_dim(branch_whole, own_start, local_rows, 0)
    output_rows = (tokens_f + branch_sum + resid_bias).astype(jnp.bfloat16)
    head_top = lax.pmax(jnp.max(block_tops, axis=0), "dp")
    factor = jnp.sqrt(clip_tau / jnp.maximum(head_top, clip_tau))
    clipped_qk = (w_qkv[:2].astype(jnp.float32) * jnp.repeat(factor, HDIM)[None, None, :]).astype(
        jnp.bfloat16
    )
    cot_full = lax.all_gather(cotangent, "tensor", axis=0, tiled=True)
    grad_attended = jnp.einsum(
        "td,hd->th", cot_full, out_w, preferred_element_type=jnp.float32
    ).astype(jnp.bfloat16)
    grad_w_out = jnp.einsum("th,td->hd", attended, cot_full, preferred_element_type=jnp.float32)
    grad_act = jnp.einsum("td,fd->tf", cot_full, down_w, preferred_element_type=jnp.float32)
    ignored, gelu_back = jax.vjp(gelu_tanh, hidden_pre)
    grad_hidden = gelu_back(grad_act)[0].astype(jnp.bfloat16)
    grad_w_fc2 = jnp.einsum("tf,td->fd", activated, cot_full, preferred_element_type=jnp.float32)
    grad_w_fc1 = jnp.einsum("td,tf->df", normed, grad_hidden, preferred_element_type=jnp.float32)
    grad_b_fc1 = jnp.sum(grad_hidden.astype(jnp.float32), axis=0)
    grad_heads = grad_attended.reshape(total_rows, head_count, HDIM)

    def back_block(carry, block_pair):
        grad_keys, grad_values = carry
        row_start, log_rows = block_pair
        query_rows = lax.dynamic_slice_in_dim(queries, row_start, QBLK, 0)
        grad_rows = lax.dynamic_slice_in_dim(grad_heads, row_start, QBLK, 0)
        raw_scores = (
            jnp.einsum("qhe,khe->hqk", query_rows, keys_rot, preferred_element_type=jnp.float32)
            * score_scale
        )
        allowed = block_mask(ancestry, row_start, QBLK, total_rows, SEG)
        masked = jnp.where(allowed[None], raw_scores, -1e30)
        probs_f = jnp.exp(masked - log_rows[..., None])
        probs_low = probs_f.astype(jnp.bfloat16)
        grad_probs = jnp.einsum(
            "qhe,khe->hqk", grad_rows, values_all, preferred_element_type=jnp.float32
        )
        grad_scores = (
            probs_f * (grad_probs - jnp.sum(probs_f * grad_probs, axis=2, keepdims=True))
        ).astype(jnp.bfloat16)
        grad_queries = (
            jnp.einsum("hqk,khe->qhe", grad_scores, keys_rot, preferred_element_type=jnp.float32)
            * score_scale
        )
        grad_keys = (
            grad_keys
            + jnp.einsum(
                "hqk,qhe->khe", grad_scores, query_rows, preferred_element_type=jnp.float32
            )
            * score_scale
        )
        grad_values = grad_values + jnp.einsum(
            "hqk,qhe->khe", probs_low, grad_rows, preferred_element_type=jnp.float32
        )
        return ((grad_keys, grad_values), grad_queries)

    zero_heads = jnp.zeros((total_rows, head_count, HDIM), jnp.float32)
    (grad_keys, grad_values), grad_queries = lax.scan(
        back_block, (zero_heads, zero_heads), (block_starts, log_totals)
    )
    grad_queries = grad_queries.reshape(total_rows, head_count, HDIM)
    grad_qkv = jnp.stack(
        [
            unrotate(grad_queries, cos_rows, sin_rows),
            unrotate(grad_keys, cos_rows, sin_rows),
            grad_values,
        ]
    )
    grad_qkv = grad_qkv.reshape(3, total_rows, head_count * HDIM).astype(jnp.bfloat16)
    grad_w_qkv = jnp.einsum("td,cth->cdh", normed, grad_qkv, preferred_element_type=jnp.float32)
    grad_b_qkv = jnp.sum(grad_qkv.astype(jnp.float32), axis=1)
    summed_qkv, summed_out, summed_fc1, summed_fc2 = (
        lax.psum_scatter(
            grad_w_qkv.astype(jnp.bfloat16), "dp", scatter_dimension=1, tiled=True
        ).astype(jnp.float32),
        lax.psum_scatter(
            grad_w_out.astype(jnp.bfloat16), "dp", scatter_dimension=1, tiled=True
        ).astype(jnp.float32),
        lax.psum_scatter(
            grad_w_fc1.astype(jnp.bfloat16), "dp", scatter_dimension=0, tiled=True
        ).astype(jnp.float32),
        lax.psum_scatter(
            grad_w_fc2.astype(jnp.bfloat16), "dp", scatter_dimension=1, tiled=True
        ).astype(jnp.float32),
    )
    bias_qkv, bias_fc1 = lax.psum((grad_b_qkv, grad_b_fc1), "dp")
    normed_all = lax.psum(
        (
            jnp.einsum("cth,cdh->td", grad_qkv, qkv_w, preferred_element_type=jnp.float32)
            + jnp.einsum("tf,df->td", grad_hidden, up_w, preferred_element_type=jnp.float32)
        ).astype(jnp.bfloat16),
        "tensor",
    ).astype(jnp.float32)
    grad_normed = lax.dynamic_slice_in_dim(normed_all, own_start, local_rows, 0)
    ignored_rows, norm_back = jax.vjp(norm_rows, tokens_f, ln_gain, ln_bias)
    grad_tokens, gain_part, shift_part = norm_back(grad_normed)
    cot_local = cotangent.astype(jnp.float32)
    input_grad = cot_local + grad_tokens
    small_terms = jnp.stack([gain_part, shift_part, jnp.sum(cot_local, axis=0)])
    grad_small = lax.psum_scatter(small_terms, ("dp", "tensor"), scatter_dimension=1, tiled=True)
    return (
        output_rows,
        input_grad,
        grad_small,
        summed_qkv,
        bias_qkv,
        summed_out,
        summed_fc1,
        bias_fc1,
        summed_fc2,
        clipped_qk,
    )


def solution(mesh):
    return jax.shard_map(
        body,
        mesh=mesh,
        in_specs=(
            P(("dp", "tensor"), None),
            P(("dp", "tensor"), None),
            P(),
            P(),
            P(None, "dp", "tensor"),
            P(None, "tensor"),
            P("tensor", "dp"),
            P("dp", "tensor"),
            P("tensor"),
            P("tensor", "dp"),
            P(),
            P("dp", None),
        ),
        out_specs=(
            P(("dp", "tensor"), None),
            P(("dp", "tensor"), None),
            P(None, ("dp", "tensor")),
            P(None, "dp", "tensor"),
            P(None, "tensor"),
            P("tensor", "dp"),
            P("dp", "tensor"),
            P("tensor"),
            P("tensor", "dp"),
            P(None, "dp", "tensor"),
        ),
        check_vma=False,
    )
```

profile of v0, /device:TPU:0, one launch (start us, length us, event | category | flops | bytes accessed | tf_op | source)
XLA Modules:
  0.0 2248.9 jit_solution(18235470847636643022)
XLA Ops:
  21.2 56.9 %all-gather.9.cloned.1.call-done = bf16[3,2048,512]{1,2,0:T(8,128)(2,1)} async-done(((bf16[3,256,512]{1,2,0:T(8,128)(2,1)}), bf16[3,2048,512]{1,2,0:T(8,128)(2,1)}) %all-gather.9.cloned.1.call-update) | async-done | bytes 6291472 | tf_op jit(solution)/shard_map/all_gather | solution.py:117
  78.1 96.4 %all-gather.7.cloned.1.call-done = bf16[2304,2048]{1,0:T(8,128)(2,1)} async-done(((bf16[576,2048]{1,0:T(8,128)(2,1)}), bf16[2304,2048]{1,0:T(8,128)(2,1)}) %all-gather.7.cloned.1.call-update) | async-done | bytes 9437200 | tf_op jit(solution)/shard_map/all_gather | solution.py:122
  207.6 261.1 %while.35 = (s32[]{:T(128)}, bf16[3,768,8,64]{1,3,2,0:T(8,128)(2,1)}, f32[3,8,768]{2,1,0:T(8,128)}, f32[3,8]{1,0:T(4,128)}, s32[3]{0:T(128)S(1)}, /*index=5*/pre...) while((s32[]{:T(128)}, ...), condition=%wide.region_24.25_spmd, body=%wide.region_20.24_spmd.sunk | while | flops 3817168896 | bytes 187103536 | solution.py:149
  479.2 657.4 %while.36 = (s32[]{:T(128)}, f32[2304,8,64]{0,2,1:T(8,128)}, f32[2304,8,64]{0,2,1:T(8,128)}, f32[3,768,8,64]{1,0,3,2:T(4,128)}, s32[3]{0:T(128)S(1)}, /*index=5*...) while((s32[]{:T(128)}, f32[2304,8,64]{0,2,1:T(8,128)}, ...), condition=%wide.region_28.29_spmd.clone, body=%wide.region_26.28_spmd.clone.sunk | while | flops 9287196672 | bytes 472552672 | solution.py:214
  529.8 42.9 %multiply_reduce_fusion.2 = (f32[8,768]{1,0:T(8,128)S(1)}, f32[8,768,2304]{2,1,0:T(8,128)}) fusion(f32[8,768,2304]{2,1,0:T(8,128)} %fusion.183, f32[8,768]{1,0:T(8,128)S(1)} %dynamic-slice_bitcast_fusion.2, pred[768,2304]{1,0:T(8,128)(4,1)S(1)} %copy.77, bf16[2304,8,64]{0,2,1:T(8,128)(2,1)} %get-tuple-element.715, ...), kind=kOutput, calls=%fused_computation.38.clone.1 | convolution fusion | flops 1882712064 | bytes 118210560 | tf_op jit(solution)/shard_map/while/body/eval_jaxpr/qhe,khe->hqk/dot_general | solution.py:191
  572.7 44.8 %multiply_convert_fusion.6 = bf16[8,768,2304]{2,1,0:T(8,128)(2,1)} fusion(f32[8,768,2304]{2,1,0:T(8,128)} %get-tuple-element.614, f32[8,768,2304]{2,1,0:T(8,128)} %fusion.183, f32[8,768]{1,0:T(8,128)S(1)} %get-tuple-element.615, f32[8,768]{1,0:T(8,128)S(1)} %dynamic-slice_bitcast_fusion.2, pred[768,2304]{1,0:T(8,128)(4,1)S(1)} %copy.77), kind=kLoop, calls=%fused_computation.37.clone.1 | loop fusion | flops 84934656 | bytes 143376384 | tf_op jit(solution)/shard_map/while/body/eval_jaxpr/convert_element_type | solution.py:196
  634.2 30.3 %dynamic_update_slice.42 = f32[3,768,8,64]{1,0,3,2:T(4,128)} dynamic-update-slice(f32[3,768,8,64]{1,0,3,2:T(4,128)} %get-tuple-element.689, f32[1,768,8,64]{1,0,3,2:T(1,128)} %copy.78, s32[]{:T(128)} %get-tuple-element.686, s32[]{:T(128)} %constant.247.clone.1..sunk.1, s32[]{:T(128)} %constant.247.clone.1..sunk.1, s32[]{:T(128)} %constant.247.clone.1..sunk.1) | dynamic-update-slice | bytes 3145732 | tf_op jit(solution)/shard_map/while/body/jit(dynamic_update_index_in_dim)/dynamic_update_slice | solution.py:214
  741.9 42.9 %multiply_reduce_fusion.2 = (f32[8,768]{1,0:T(8,128)S(1)}, f32[8,768,2304]{2,1,0:T(8,128)}) fusion(f32[8,768,2304]{2,1,0:T(8,128)} %fusion.183, f32[8,768]{1,0:T(8,128)S(1)} %dynamic-slice_bitcast_fusion.2, pred[768,2304]{1,0:T(8,128)(4,1)S(1)} %copy.77, bf16[2304,8,64]{0,2,1:T(8,128)(2,1)} %get-tuple-element.715, ...), kind=kOutput, calls=%fused_computation.38.clone.1 | convolution fusion | flops 1882712064 | bytes 118210560 | tf_op jit(solution)/shard_map/while/body/eval_jaxpr/qhe,khe->hqk/dot_general | solution.py:191
  784.8 44.8 %multiply_convert_fusion.6 = bf16[8,768,2304]{2,1,0:T(8,128)(2,1)} fusion(f32[8,768,2304]{2,1,0:T(8,128)} %get-tuple-element.614, f32[8,768,2304]{2,1,0:T(8,128)} %fusion.183, f32[8,768]{1,0:T(8,128)S(1)} %get-tuple-element.615, f32[8,768]{1,0:T(8,128)S(1)} %dynamic-slice_bitcast_fusion.2, pred[768,2304]{1,0:T(8,128)(4,1)S(1)} %copy.77), kind=kLoop, calls=%fused_computation.37.clone.1 | loop fusion | flops 84934656 | bytes 143376384 | tf_op jit(solution)/shard_map/while/body/eval_jaxpr/convert_element_type | solution.py:196
  846.3 30.3 %dynamic_update_slice.42 = f32[3,768,8,64]{1,0,3,2:T(4,128)} dynamic-update-slice(f32[3,768,8,64]{1,0,3,2:T(4,128)} %get-tuple-element.689, f32[1,768,8,64]{1,0,3,2:T(1,128)} %copy.78, s32[]{:T(128)} %get-tuple-element.686, s32[]{:T(128)} %constant.247.clone.1..sunk.1, s32[]{:T(128)} %constant.247.clone.1..sunk.1, s32[]{:T(128)} %constant.247.clone.1..sunk.1) | dynamic-update-slice | bytes 3145732 | tf_op jit(solution)/shard_map/while/body/jit(dynamic_update_index_in_dim)/dynamic_update_slice | solution.py:214
  956.7 42.9 %multiply_reduce_fusion.2 = (f32[8,768]{1,0:T(8,128)S(1)}, f32[8,768,2304]{2,1,0:T(8,128)}) fusion(f32[8,768,2304]{2,1,0:T(8,128)} %fusion.183, f32[8,768]{1,0:T(8,128)S(1)} %dynamic-slice_bitcast_fusion.2, pred[768,2304]{1,0:T(8,128)(4,1)S(1)} %copy.77, bf16[2304,8,64]{0,2,1:T(8,128)(2,1)} %get-tuple-element.715, ...), kind=kOutput, calls=%fused_computation.38.clone.1 | convolution fusion | flops 1882712064 | bytes 118210560 | tf_op jit(solution)/shard_map/while/body/eval_jaxpr/qhe,khe->hqk/dot_general | solution.py:191
  999.6 44.8 %multiply_convert_fusion.6 = bf16[8,768,2304]{2,1,0:T(8,128)(2,1)} fusion(f32[8,768,2304]{2,1,0:T(8,128)} %get-tuple-element.614, f32[8,768,2304]{2,1,0:T(8,128)} %fusion.183, f32[8,768]{1,0:T(8,128)S(1)} %get-tuple-element.615, f32[8,768]{1,0:T(8,128)S(1)} %dynamic-slice_bitcast_fusion.2, pred[768,2304]{1,0:T(8,128)(4,1)S(1)} %copy.77), kind=kLoop, calls=%fused_computation.37.clone.1 | loop fusion | flops 84934656 | bytes 143376384 | tf_op jit(solution)/shard_map/while/body/eval_jaxpr/convert_element_type | solution.py:196
  1061.1 30.3 %dynamic_update_slice.42 = f32[3,768,8,64]{1,0,3,2:T(4,128)} dynamic-update-slice(f32[3,768,8,64]{1,0,3,2:T(4,128)} %get-tuple-element.689, f32[1,768,8,64]{1,0,3,2:T(1,128)} %copy.78, s32[]{:T(128)} %get-tuple-element.686, s32[]{:T(128)} %constant.247.clone.1..sunk.1, s32[]{:T(128)} %constant.247.clone.1..sunk.1, s32[]{:T(128)} %constant.247.clone.1..sunk.1) | dynamic-update-slice | bytes 3145732 | tf_op jit(solution)/shard_map/while/body/jit(dynamic_update_index_in_dim)/dynamic_update_slice | solution.py:214
  1211.5 39.5 %convert_reduce_fusion = (f32[2048]{0:T(1024)}, bf16[2304,2048]{1,0:T(8,128)(2,1)}) fusion(f32[2304,2048]{1,0:T(8,128)} %fusion.123, f32[2048]{0:T(1024)S(1)} %copy-done.25, bf16[2304,2048]{1,0:T(8,128)(2,1)} %all-gather.17.cloned.1.call-done, bf16[2048,2048]{1,0:T(8,128)(2,1)} %all-gather.15.cloned.1.call-done), kind=kOutput, calls=%fused_computation.94 | convolution fusion | flops 19435878400 | bytes 46153728 | tf_op jit(solution)/shard_map/td,fd->tf/dot_general | solution.py:170
  1251.1 28.0 %fusion.59 = bf16[2304,2048]{1,0:T(8,128)(2,1)} fusion(f32[2304,2048,1]{1,0,2:T(8,128)} %fusion.119, bf16[2304,2048]{1,0:T(8,128)(2,1)} %get-tuple-element.444, bf16[2048,2048]{1,0:T(8,128)(2,1)} %all-gather.13.cloned.1.call-done), kind=kOutput, calls=%fused_computation.93 | convolution fusion | flops 19336790016 | bytes 46137344 | tf_op jit(solution)/shard_map/tf,df->td/dot_general | solution.py:246
  1294.2 32.4 %convolution_add_fusion = f32[2304,2048]{1,0:T(8,128)} fusion(f32[2304,2048]{1,0:T(8,128)} %fusion.122, bf16[2048,2048]{1,0:T(8,128)(2,1)} %all-gather.15.cloned.1.call-done, f32[2304,2048]{1,0:T(8,128)} %fusion.123, f32[2048]{0:T(1024)S(1)} %copy-done.25), kind=kOutput, calls=%fused_computation.98 | convolution fusion | flops 19379257344 | bytes 65019904 | tf_op jit(solution)/shard_map/dot_general | solution.py:155
  1384.7 31.1 %convolution_convert_fusion = bf16[2048,2048]{1,0:T(8,128)(2,1)} fusion(bf16[2304,2048]{1,0:T(8,128)(2,1)} %all-gather.17.cloned.1.call-done, f32[2304,2048]{1,0:T(8,128)} %fusion.123, f32[2048]{0:T(1024)S(1)} %copy-done.25), kind=kOutput, calls=%fused_computation.103 | convolution fusion | flops 19378733056 | bytes 36708352 | tf_op jit(solution)/shard_map/tf,td->fd/dot_general | solution.py:173
  1437.2 30.7 %all-reduce.6.cloned.1.call-done = bf16[2304,2048]{1,0:T(8,128)(2,1)} async-done(((bf16[2304,2048]{1,0:T(8,128)(2,1)}), bf16[2304,2048]{1,0:T(8,128)(2,1)}) %all-reduce.6.cloned.1.call-update) | async-done | bytes 9437200 | tf_op jit(solution)/shard_map/psum | solution.py:243
  1474.5 338.8 %all-reduce.4.cloned.1.call-done = f32[2304,2048]{1,0:T(8,128)} async-done(((f32[2304,2048]{1,0:T(8,128)}), f32[2304,2048]{1,0:T(8,128)}) %all-reduce.4.cloned.1.call-update) | async-done | bytes 18874384 | tf_op jit(solution)/shard_map/psum | solution.py:153
  1823.4 29.3 %all-reduce = (f32[3,512]{1,0:T(4,128)}, f32[2048]{0:T(1024)}) all-reduce(f32[3,512]{1,0:T(4,128)S(1)} %convert_reduce_fusion.1, f32[2048]{0:T(1024)S(1)} %copy-done.21), channel_id=1, replica_groups=mesh['dp'=8,'tensor'=4] {'dp'}, use_global_device_ids=true, to_apply=%region_38.39 | all-reduce | flops 3584 | bytes 28672 | tf_op jit(solution)/shard_map/psum | solution.py:242
  1855.2 69.3 %reduce-scatter.8.cloned.1.call-done = bf16[3,256,512]{1,2,0:T(8,128)(2,1)} async-done(((bf16[3,2048,512]{1,2,0:T(8,128)(2,1)}), bf16[3,256,512]{1,2,0:T(8,128)(2,1)}) %reduce-scatter.8.cloned.1.call-update) | async-done | bytes 786448 | tf_op jit(solution)/shard_map/reduce_scatter | solution.py:229
  1927.0 87.8 %reduce-scatter.12.cloned.1.call-done = bf16[256,2048]{1,0:T(8,128)(2,1)} async-done(((bf16[2048,2048]{1,0:T(8,128)(2,1)}), bf16[256,2048]{1,0:T(8,128)(2,1)}) %reduce-scatter.12.cloned.1.call-update) | async-done | bytes 1048592 | tf_op jit(solution)/shard_map/reduce_scatter | solution.py:235
  2017.6 87.4 %reduce-scatter.14.cloned.1.call-done = bf16[2048,256]{1,0:T(8,128)(2,1)} async-done(((bf16[2048,2048]{1,0:T(8,128)(2,1)}), bf16[2048,256]{1,0:T(8,128)(2,1)}) %reduce-scatter.14.cloned.1.call-update) | async-done | bytes 1048592 | tf_op jit(solution)/shard_map/reduce_scatter | solution.py:238
  2107.8 133.0 %reduce-scatter.16.cloned.1.call-done = f32[64,3]{1,0:T(8,128)} async-done(((f32[2048,3]{1,0:T(8,128)}), f32[64,3]{1,0:T(8,128)}) %reduce-scatter.16.cloned.1.call-update) | async-done | bytes 784
  (253 shorter events, 769.0 us)
Async XLA Ops:
  7.2 70.9 %all-gather.9.cloned.1.call-start = ((), (), s32[]{:S(2)}) async-start(), calls=%async_computation.6 | async-start | bytes 7077888 | tf_op jit(solution)/shard_map/all_gather | solution.py:117
  9.7 164.8 %all-gather.7.cloned.1.call-start = ((), (), s32[]{:S(2)}) async-start(), calls=%async_computation.5 | async-start | bytes 11796480 | tf_op jit(solution)/shard_map/all_gather | solution.py:122
  16.2 158.4 %copy-start.24 = (f32[3,512]{1,0:T(4,128)S(1)}, f32[3,512]{1,0:T(4,128)}, u32[]{:S(2)}) copy-start(f32[3,512]{1,0:T(4,128)} %param.21) | copy-start | bytes 18436
  16.2 452.5 %all-gather.11.cloned.1.call-start = ((), (), s32[]{:S(2)}) async-start(), calls=%async_computation.7 | async-start | bytes 2359296 | tf_op jit(solution)/shard_map/all_gather | solution.py:118
  16.9 451.8 %all-gather.17.cloned.1.call-start = ((), (), s32[]{:S(2)}) async-start(), calls=%async_computation.11 | async-start | bytes 11796480 | tf_op jit(solution)/shard_map/all_gather | solution.py:165
  17.5 1167.6 %all-gather.13.cloned.1.call-start = ((), (), s32[]{:S(2)}) async-start(), calls=%async_computation.8 | async-start | bytes 9437184 | tf_op jit(solution)/shard_map/all_gather | solution.py:119
  18.1 1193.4 %all-gather.15.cloned.1.call-start = ((), (), s32[]{:S(2)}) async-start(), calls=%async_computation.9 | async-start | bytes 9437184 | tf_op jit(solution)/shard_map/all_gather | solution.py:120
  18.7 1449.3 %all-reduce.6.cloned.1.call-start = ((), (), s32[]{:S(2)}) async-start(), calls=%async_computation.12 | async-start | bytes 18874368 | tf_op jit(solution)/shard_map/psum | solution.py:243
  21.2 183.4 %copy-start.7 = (f32[2304,16]{0,1:T(8,128)}, f32[2304,16]{0,1:T(8,128)S(1)}, u32[]{:S(2)}) copy-start(f32[2304,16]{0,1:T(8,128)S(1)} %get-tuple-element.470) | copy-start | bytes 442372
  21.2 183.3 %copy-start.9 = (f32[2304,16]{0,1:T(8,128)}, f32[2304,16]{0,1:T(8,128)S(1)}, u32[]{:S(2)}) copy-start(f32[2304,16]{0,1:T(8,128)S(1)} %get-tuple-element.471) | copy-start | bytes 442372
  1279.1 534.1 %all-reduce.4.cloned.1.call-start = ((), (), s32[]{:S(2)}) async-start(), calls=%async_computation.10 | async-start | bytes 37748736 | tf_op jit(solution)/shard_map/psum | solution.py:153
  1326.7 526.7 %reduce-scatter.10.cloned.1.call-start = ((), (), s32[]{:S(2)}) async-start(), calls=%async_computation.14 | async-start | bytes 2359296 | tf_op jit(solution)/shard_map/reduce_scatter | solution.py:232
  1336.2 588.3 %reduce-scatter.8.cloned.1.call-start = ((), (), s32[]{:S(2)}) async-start(), calls=%async_computation.13 | async-start | bytes 7077888 | tf_op jit(solution)/shard_map/reduce_scatter | solution.py:229
  1357.9 656.9 %reduce-scatter.12.cloned.1.call-start = ((), (), s32[]{:S(2)}) async-start(), calls=%async_computation.15 | async-start | bytes 9437184 | tf_op jit(solution)/shard_map/reduce_scatter | solution.py:235
  1384.6 720.5 %reduce-scatter.14.cloned.1.call-start = ((), (), s32[]{:S(2)}) async-start(), calls=%async_computation.16 | async-start | bytes 9437184 | tf_op jit(solution)/shard_map/reduce_scatter | solution.py:238
  1415.8 52.2 %copy-start.2 = (bf16[576,2048]{1,0:T(8,128)(2,1)S(1)}, bf16[576,2048]{1,0:T(8,128)(2,1)}, u32[]{:S(2)}) copy-start(bf16[576,2048]{1,0:T(8,128)(2,1)} %param.16) | copy-start | bytes 7077892
  1415.8 52.2 %copy-start.12 = (f32[576]{0:T(1024)S(1)}, f32[576]{0:T(1024)}, u32[]{:S(2)}) copy-start(f32[576]{0:T(1024)} %copy-done.11) | copy-start | bytes 6916
  1415.8 52.2 %copy-start.14 = (f32[2048]{0:T(1024)S(1)}, f32[2048]{0:T(1024)}, u32[]{:S(2)}) copy-start(f32[2048]{0:T(1024)} %param.18) | copy-start | bytes 24580
  1415.8 824.9 %reduce-scatter.16.cloned.1.call-start = ((), (), s32[]{:S(2)}) async-start(), calls=%async_computation.17 | async-start | bytes 1081344
  1433.1 37.6 %copy-start.18 = (f32[576]{0:T(1024)S(1)}, f32[576]{0:T(1024)}, u32[]{:S(2)}) copy-start(f32[576]{0:T(1024)} %copy-done.17) | copy-start | bytes 6916
  1433.1 37.6 %copy-start.16 = (f32[576]{0:T(1024)S(1)}, f32[576]{0:T(1024)}, u32[]{:S(2)}) copy-start(f32[576]{0:T(1024)} %copy-done.15) | copy-start | bytes 6916
  1437.2 376.1 %copy-start.19 = (f32[2048]{0:T(1024)S(1)}, f32[2048]{0:T(1024)}, u32[]{:S(2)}) copy-start(f32[2048]{0:T(1024)} %param.26) | copy-start | bytes 24580
  1474.5 348.0 %copy-start.6 = (bf16[3,256,512]{2,1,0:T(8,128)(2,1)S(1)}, bf16[3,256,512]{2,1,0:T(8,128)(2,1)}, u32[]{:S(2)}) copy-start(bf16[3,256,512]{2,1,0:T(8,128)(2,1)} %param.20) | copy-start | bytes 2359300
  1474.5 348.9 %copy-start.21 = (f32[2048]{0:T(1024)S(1)}, f32[2048]{0:T(1024)}, u32[]{:S(2)}) copy-start(f32[2048]{0:T(1024)} %get-tuple-element.443) | copy-start | bytes 24580
  (16 other events, 95.5 us)
Sparse Core Ops, SparseCore 0:
  10.2 67.8 all-gather.8
  80.0 94.5 all-gather.6
  176.2 30.8 all-gather.10
  208.7 95.3 all-gather.16
  305.6 82.0 all-gather.12
  389.1 81.0 all-gather.14
  1279.2 188.6 all-reduce.5
  1471.5 341.7 all-reduce.3
  1816.2 37.0 reduce-scatter.9
  1855.6 68.7 reduce-scatter.7
  1926.9 87.9 reduce-scatter.11
  2017.1 87.9 reduce-scatter.13
  2107.4 133.2 reduce-scatter.15
where the time goes:
time: 2260 us; the launch traced here: 2250 us
  waiting for transfers between devices  903 us (40%)
  matrix products  798 us (35%)
  other arithmetic  263 us (12%)
  local copies, waits for them, and re-layouts  174 us (8%)
  loops' own time  50.7 us (2%)
  blocking collectives  45.8 us (2%)
    psum x1, waiting for transfers between devices, body(): lax.psum(jnp.dot(attended, out_w, preferred_element_type=jnp.float32) + j...  339 us
    unnamed x14, waiting for transfers between devices  135 us
    convert_element_type x3, other arithmetic, back_block(): grad_scores = (probs_f * (grad_probs - jnp.sum(probs_f * grad_probs, axis...  134 us
    dot_general x3, matrix products, back_block(): jnp.einsum('qhe,khe->hqk', grad_rows, values_all, preferred_element_type=...  129 us
    dynamic_update_slice x6, local copies, waits for them, and re-layouts, body(): lax.scan(back_block, (zero_heads, zero_heads), (block_starts, log_totals))  99.3 us
    all_gather x1, waiting for transfers between devices, body(): normed = lax.all_gather(normed_local, 'tensor', axis=0, tiled=True)  96.4 us
    reduce_scatter x1, waiting for transfers between devices, body(): lax.psum_scatter(grad_w_fc1.astype(jnp.bfloat16), 'dp', scatter_dimension...  87.8 us
    reduce_scatter x1, waiting for transfers between devices, body(): lax.psum_scatter(grad_w_fc2.astype(jnp.bfloat16), 'dp', scatter_dimension...  87.4 us
  transfers between devices with their start and end apart: 13, of which 9 were waited for; matrix products, arithmetic and copies ran while one was open for 51% of the time, Pallas kernels for 0%

commit v1 on v0

--- a/solution.py
+++ b/solution.py
@@ -150,11 +150,11 @@
     attended = attended.reshape(total_rows, head_count * HDIM)
     hidden_pre = jnp.dot(normed, up_w, preferred_element_type=jnp.float32) + b_fc1
     activated = gelu_tanh(hidden_pre).astype(jnp.bfloat16)
-    branch_whole = lax.psum(
-        jnp.dot(attended, out_w, preferred_element_type=jnp.float32)
-        + jnp.dot(activated, down_w, preferred_element_type=jnp.float32),
-        "tensor",
-    )
+    x = jnp.dot(attended, out_w, preferred_element_type=jnp.float32) + jnp.dot(
+        activated, down_w, preferred_element_type=jnp.float32
+    )
+    parts = lax.all_gather(x, "tensor")
+    branch_whole = jnp.sum(parts, axis=0)
     branch_sum = lax.dynamic_slice_in_dim(branch_whole, own_start, local_rows, 0)
     output_rows = (tokens_f + branch_sum + resid_bias).astype(jnp.bfloat16)
     head_top = lax.pmax(jnp.max(block_tops, axis=0), "dp")

time: 2260 us -> 2560 us (1.13)
  waiting for transfers between devices: 903 us -> 1170 us
  other arithmetic: 263 us -> 294 us
    all_gather x0 -> x1, waiting for transfers between devices: none -> 642 us  [body(): parts = lax.all_gather(x, 'tensor')]
    psum x1 -> x0, waiting for transfers between devices: 339 us -> none  [body(): lax.psum(jnp.dot(attended, out_w, preferred_element_type=jnp.float32) + j...]
    reduce_scatter x1, waiting for transfers between devices: 69.3 us -> 36.2 us  [body(): lax.psum_scatter(grad_w_qkv.astype(jnp.bfloat16), 'dp', scatter_dimension...]
    reduce_sum x0 -> x1, other arithmetic: none -> 31.3 us  [body(): branch_whole = jnp.sum(parts, axis=0)]
  transfers between devices with their start and end apart: 13 -> 13, of which waited for: 9 -> 8; matrix products, arithmetic and copies ran while one was open for 51% -> 47% of each run, Pallas kernels for 0% -> 0%
where the time goes in v1:
time: 2560 us; the launch traced here: 2550 us
  waiting for transfers between devices  1170 us (46%)
  matrix products  798 us (31%)
  other arithmetic  294 us (11%)
  local copies, waits for them, and re-layouts  173 us (7%)
  loops' own time  50.7 us (2%)
  blocking collectives  47.1 us (2%)
    all_gather x1, waiting for transfers between devices, body(): parts = lax.all_gather(x, 'tensor')  642 us
    unnamed x14, waiting for transfers between devices  135 us
    convert_element_type x3, other arithmetic, back_block(): grad_scores = (probs_f * (grad_probs - jnp.sum(probs_f * grad_probs, axis...  134 us
    dot_general x3, matrix products, back_block(): jnp.einsum('qhe,khe->hqk', grad_rows, values_all, preferred_element_type=...  129 us
    dynamic_update_slice x6, local copies, waits for them, and re-layouts, body(): lax.scan(back_block, (zero_heads, zero_heads), (block_starts, log_totals))  99.3 us
    all_gather x1, waiting for transfers between devices, body(): normed = lax.all_gather(normed_local, 'tensor', axis=0, tiled=True)  96.4 us
    reduce_scatter x1, waiting for transfers between devices, body(): lax.psum_scatter(grad_w_fc1.astype(jnp.bfloat16), 'dp', scatter_dimension...  87.7 us
    reduce_scatter x1, waiting for transfers between devices, body(): lax.psum_scatter(grad_w_fc2.astype(jnp.bfloat16), 'dp', scatter_dimension...  87.3 us
  transfers between devices with their start and end apart: 13, of which 8 were waited for; matrix products, arithmetic and copies ran while one was open for 47% of the time, Pallas kernels for 0%

profile of v1, /device:TPU:0, one launch (start us, length us, event | category | flops | bytes accessed | tf_op | source)
XLA Modules:
  0.0 2550.8 jit_solution(13124576986834934755)
XLA Ops:
  21.2 56.9 %all-gather.11.cloned.1.call-done = bf16[3,2048,512]{1,2,0:T(8,128)(2,1)} async-done(((bf16[3,256,512]{1,2,0:T(8,128)(2,1)}), bf16[3,2048,512]{1,2,0:T(8,128)(2,1)}) %all-gather.11.cloned.1.call-update) | async-done | bytes 6291472 | tf_op jit(solution)/shard_map/all_gather | solution.py:117
  78.1 96.4 %all-gather.9.cloned.1.call-done = bf16[2304,2048]{1,0:T(8,128)(2,1)} async-done(((bf16[576,2048]{1,0:T(8,128)(2,1)}), bf16[2304,2048]{1,0:T(8,128)(2,1)}) %all-gather.9.cloned.1.call-update) | async-done | bytes 9437200 | tf_op jit(solution)/shard_map/all_gather | solution.py:122
  207.6 261.1 %while.35 = (s32[]{:T(128)}, bf16[3,768,8,64]{1,3,2,0:T(8,128)(2,1)}, f32[3,8,768]{2,1,0:T(8,128)}, f32[3,8]{1,0:T(4,128)}, s32[3]{0:T(128)S(1)}, /*index=5*/pre...) while((s32[]{:T(128)}, ...), condition=%wide.region_24.25_spmd, body=%wide.region_20.24_spmd.sunk | while | flops 3817168896 | bytes 187103536 | solution.py:149
  479.2 657.4 %while.36 = (s32[]{:T(128)}, f32[2304,8,64]{0,2,1:T(8,128)}, f32[2304,8,64]{0,2,1:T(8,128)}, f32[3,768,8,64]{1,0,3,2:T(4,128)}, s32[3]{0:T(128)S(1)}, /*index=5*...) while((s32[]{:T(128)}, f32[2304,8,64]{0,2,1:T(8,128)}, ...), condition=%wide.region_28.29_spmd.clone, body=%wide.region_26.28_spmd.clone.sunk | while | flops 9287196672 | bytes 472552672 | solution.py:214
  529.8 42.9 %multiply_reduce_fusion.2 = (f32[8,768]{1,0:T(8,128)S(1)}, f32[8,768,2304]{2,1,0:T(8,128)}) fusion(f32[8,768,2304]{2,1,0:T(8,128)} %fusion.183, f32[8,768]{1,0:T(8,128)S(1)} %dynamic-slice_bitcast_fusion.2, pred[768,2304]{1,0:T(8,128)(4,1)S(1)} %copy.78, bf16[2304,8,64]{0,2,1:T(8,128)(2,1)} %get-tuple-element.715, ...), kind=kOutput, calls=%fused_computation.38.clone.1 | convolution fusion | flops 1882712064 | bytes 118210560 | tf_op jit(solution)/shard_map/while/body/eval_jaxpr/qhe,khe->hqk/dot_general | solution.py:191
  572.7 44.8 %multiply_convert_fusion.6 = bf16[8,768,2304]{2,1,0:T(8,128)(2,1)} fusion(f32[8,768,2304]{2,1,0:T(8,128)} %get-tuple-element.614, f32[8,768,2304]{2,1,0:T(8,128)} %fusion.183, f32[8,768]{1,0:T(8,128)S(1)} %get-tuple-element.615, f32[8,768]{1,0:T(8,128)S(1)} %dynamic-slice_bitcast_fusion.2, pred[768,2304]{1,0:T(8,128)(4,1)S(1)} %copy.78), kind=kLoop, calls=%fused_computation.37.clone.1 | loop fusion | flops 84934656 | bytes 143376384 | tf_op jit(solution)/shard_map/while/body/eval_jaxpr/convert_element_type | solution.py:196
  634.2 30.3 %dynamic_update_slice.42 = f32[3,768,8,64]{1,0,3,2:T(4,128)} dynamic-update-slice(f32[3,768,8,64]{1,0,3,2:T(4,128)} %get-tuple-element.689, f32[1,768,8,64]{1,0,3,2:T(1,128)} %copy.79, s32[]{:T(128)} %get-tuple-element.686, s32[]{:T(128)} %constant.247.clone.1..sunk.1, s32[]{:T(128)} %constant.247.clone.1..sunk.1, s32[]{:T(128)} %constant.247.clone.1..sunk.1) | dynamic-update-slice | bytes 3145732 | tf_op jit(solution)/shard_map/while/body/jit(dynamic_update_index_in_dim)/dynamic_update_slice | solution.py:214
  741.9 42.9 %multiply_reduce_fusion.2 = (f32[8,768]{1,0:T(8,128)S(1)}, f32[8,768,2304]{2,1,0:T(8,128)}) fusion(f32[8,768,2304]{2,1,0:T(8,128)} %fusion.183, f32[8,768]{1,0:T(8,128)S(1)} %dynamic-slice_bitcast_fusion.2, pred[768,2304]{1,0:T(8,128)(4,1)S(1)} %copy.78, bf16[2304,8,64]{0,2,1:T(8,128)(2,1)} %get-tuple-element.715, ...), kind=kOutput, calls=%fused_computation.38.clone.1 | convolution fusion | flops 1882712064 | bytes 118210560 | tf_op jit(solution)/shard_map/while/body/eval_jaxpr/qhe,khe->hqk/dot_general | solution.py:191
  784.8 44.8 %multiply_convert_fusion.6 = bf16[8,768,2304]{2,1,0:T(8,128)(2,1)} fusion(f32[8,768,2304]{2,1,0:T(8,128)} %get-tuple-element.614, f32[8,768,2304]{2,1,0:T(8,128)} %fusion.183, f32[8,768]{1,0:T(8,128)S(1)} %get-tuple-element.615, f32[8,768]{1,0:T(8,128)S(1)} %dynamic-slice_bitcast_fusion.2, pred[768,2304]{1,0:T(8,128)(4,1)S(1)} %copy.78), kind=kLoop, calls=%fused_computation.37.clone.1 | loop fusion | flops 84934656 | bytes 143376384 | tf_op jit(solution)/shard_map/while/body/eval_jaxpr/convert_element_type | solution.py:196
  846.3 30.3 %dynamic_update_slice.42 = f32[3,768,8,64]{1,0,3,2:T(4,128)} dynamic-update-slice(f32[3,768,8,64]{1,0,3,2:T(4,128)} %get-tuple-element.689, f32[1,768,8,64]{1,0,3,2:T(1,128)} %copy.79, s32[]{:T(128)} %get-tuple-element.686, s32[]{:T(128)} %constant.247.clone.1..sunk.1, s32[]{:T(128)} %constant.247.clone.1..sunk.1, s32[]{:T(128)} %constant.247.clone.1..sunk.1) | dynamic-update-slice | bytes 3145732 | tf_op jit(solution)/shard_map/while/body/jit(dynamic_update_index_in_dim)/dynamic_update_slice | solution.py:214
  956.7 42.9 %multiply_reduce_fusion.2 = (f32[8,768]{1,0:T(8,128)S(1)}, f32[8,768,2304]{2,1,0:T(8,128)}) fusion(f32[8,768,2304]{2,1,0:T(8,128)} %fusion.183, f32[8,768]{1,0:T(8,128)S(1)} %dynamic-slice_bitcast_fusion.2, pred[768,2304]{1,0:T(8,128)(4,1)S(1)} %copy.78, bf16[2304,8,64]{0,2,1:T(8,128)(2,1)} %get-tuple-element.715, ...), kind=kOutput, calls=%fused_computation.38.clone.1 | convolution fusion | flops 1882712064 | bytes 118210560 | tf_op jit(solution)/shard_map/while/body/eval_jaxpr/qhe,khe->hqk/dot_general | solution.py:191
  999.6 44.8 %multiply_convert_fusion.6 = bf16[8,768,2304]{2,1,0:T(8,128)(2,1)} fusion(f32[8,768,2304]{2,1,0:T(8,128)} %get-tuple-element.614, f32[8,768,2304]{2,1,0:T(8,128)} %fusion.183, f32[8,768]{1,0:T(8,128)S(1)} %get-tuple-element.615, f32[8,768]{1,0:T(8,128)S(1)} %dynamic-slice_bitcast_fusion.2, pred[768,2304]{1,0:T(8,128)(4,1)S(1)} %copy.78), kind=kLoop, calls=%fused_computation.37.clone.1 | loop fusion | flops 84934656 | bytes 143376384 | tf_op jit(solution)/shard_map/while/body/eval_jaxpr/convert_element_type | solution.py:196
  1061.0 30.3 %dynamic_update_slice.42 = f32[3,768,8,64]{1,0,3,2:T(4,128)} dynamic-update-slice(f32[3,768,8,64]{1,0,3,2:T(4,128)} %get-tuple-element.689, f32[1,768,8,64]{1,0,3,2:T(1,128)} %copy.79, s32[]{:T(128)} %get-tuple-element.686, s32[]{:T(128)} %constant.247.clone.1..sunk.1, s32[]{:T(128)} %constant.247.clone.1..sunk.1, s32[]{:T(128)} %constant.247.clone.1..sunk.1) | dynamic-update-slice | bytes 3145732 | tf_op jit(solution)/shard_map/while/body/jit(dynamic_update_index_in_dim)/dynamic_update_slice | solution.py:214
  1211.5 39.5 %convert_reduce_fusion = (f32[2048]{0:T(1024)}, bf16[2304,2048]{1,0:T(8,128)(2,1)}) fusion(f32[2304,2048]{1,0:T(8,128)} %fusion.123, f32[2048]{0:T(1024)S(1)} %copy-done.25, bf16[2304,2048]{1,0:T(8,128)(2,1)} %all-gather.19.cloned.1.call-done, bf16[2048,2048]{1,0:T(8,128)(2,1)} %all-gather.17.cloned.1.call-done), kind=kOutput, calls=%fused_computation.94 | convolution fusion | flops 19435878400 | bytes 46153728 | tf_op jit(solution)/shard_map/td,fd->tf/dot_general | solution.py:170
  1294.4 32.4 %convolution_add_fusion = f32[2304,2048]{1,0:T(8,128)} fusion(f32[2304,2048]{1,0:T(8,128)} %fusion.122, bf16[2048,2048]{1,0:T(8,128)(2,1)} %all-gather.17.cloned.1.call-done, f32[2304,2048]{1,0:T(8,128)} %fusion.123, f32[2048]{0:T(1024)S(1)} %copy-done.25), kind=kOutput, calls=%fused_computation.98 | convolution fusion | flops 19379257344 | bytes 65019904 | tf_op jit(solution)/shard_map/dot_general | solution.py:153
  1384.8 31.1 %convolution_convert_fusion = bf16[2048,2048]{1,0:T(8,128)(2,1)} fusion(bf16[2304,2048]{1,0:T(8,128)(2,1)} %all-gather.19.cloned.1.call-done, f32[2304,2048]{1,0:T(8,128)} %fusion.123, f32[2048]{0:T(1024)S(1)} %copy-done.25), kind=kOutput, calls=%fused_computation.103 | convolution fusion | flops 19378733056 | bytes 36708352 | tf_op jit(solution)/shard_map/tf,td->fd/dot_general | solution.py:173
  1437.6 30.4 %all-reduce.3.cloned.1.call-done = bf16[2304,2048]{1,0:T(8,128)(2,1)} async-done(((bf16[2304,2048]{1,0:T(8,128)(2,1)}), bf16[2304,2048]{1,0:T(8,128)(2,1)}) %all-reduce.3.cloned.1.call-update) | async-done | bytes 9437200 | tf_op jit(solution)/shard_map/psum | solution.py:243
  1474.5 642.5 %all-gather.21.cloned.1.call-done = f32[9216,2048]{1,0:T(8,128)} async-done(((f32[2304,2048]{1,0:T(8,128)}), f32[9216,2048]{1,0:T(8,128)}) %all-gather.21.cloned.1.call-update) | async-done | bytes 75497488 | tf_op jit(solution)/shard_map/all_gather | solution.py:156
  2117.0 31.3 %reduce_sum.322 = f32[2304,2048]{1,0:T(8,128)} reduce(f32[4,2304,2048]{2,1,0:T(8,128)} %bitcast.13, f32[]{:T(128)} %constant.249.clone.1), dimensions={0}, to_apply=%region_25.26 | reduce | flops 14155776 | bytes 94371840 | tf_op jit(solution)/shard_map/reduce_sum | solution.py:157
  2158.5 30.4 %all-reduce = (f32[3,512]{1,0:T(4,128)}, f32[2048]{0:T(1024)}) all-reduce(f32[3,512]{1,0:T(4,128)S(1)} %convert_reduce_fusion.1, f32[2048]{0:T(1024)S(1)} %copy-done.21), channel_id=1, replica_groups=mesh['dp'=8,'tensor'=4] {'dp'}, use_global_device_ids=true, to_apply=%region_38.39 | all-reduce | flops 3584 | bytes 28672 | tf_op jit(solution)/shard_map/psum | solution.py:242
  2190.6 36.2 %reduce-scatter.8.cloned.1.call-done = bf16[3,256,512]{1,2,0:T(8,128)(2,1)} async-done(((bf16[3,2048,512]{1,2,0:T(8,128)(2,1)}), bf16[3,256,512]{1,2,0:T(8,128)(2,1)}) %reduce-scatter.8.cloned.1.call-update) | async-done | bytes 786448 | tf_op jit(solution)/shard_map/reduce_scatter | solution.py:229
  2229.4 87.7 %reduce-scatter.12.cloned.1.call-done = bf16[256,2048]{1,0:T(8,128)(2,1)} async-done(((bf16[2048,2048]{1,0:T(8,128)(2,1)}), bf16[256,2048]{1,0:T(8,128)(2,1)}) %reduce-scatter.12.cloned.1.call-update) | async-done | bytes 1048592 | tf_op jit(solution)/shard_map/reduce_scatter | solution.py:235
  2319.9 87.3 %reduce-scatter.14.cloned.1.call-done = bf16[2048,256]{1,0:T(8,128)(2,1)} async-done(((bf16[2048,2048]{1,0:T(8,128)(2,1)}), bf16[2048,256]{1,0:T(8,128)(2,1)}) %reduce-scatter.14.cloned.1.call-update) | async-done | bytes 1048592 | tf_op jit(solution)/shard_map/reduce_scatter | solution.py:238
  2409.9 132.8 %reduce-scatter.16.cloned.1.call-done = f32[64,3]{1,0:T(8,128)} async-done(((f32[2048,3]{1,0:T(8,128)}), f32[64,3]{1,0:T(8,128)}) %reduce-scatter.16.cloned.1.call-update) | async-done | bytes 784
  (254 shorter events, 796.7 us)
Async XLA Ops:
  7.2 70.9 %all-gather.11.cloned.1.call-start = ((), (), s32[]{:S(2)}) async-start(), calls=%async_computation.6 | async-start | bytes 7077888 | tf_op jit(solution)/shard_map/all_gather | solution.py:117
  9.7 164.8 %all-gather.9.cloned.1.call-start = ((), (), s32[]{:S(2)}) async-start(), calls=%async_computation.5 | async-start | bytes 11796480 | tf_op jit(solution)/shard_map/all_gather | solution.py:122
  16.2 158.4 %copy-start.24 = (f32[3,512]{1,0:T(4,128)S(1)}, f32[3,512]{1,0:T(4,128)}, u32[]{:S(2)}) copy-start(f32[3,512]{1,0:T(4,128)} %param.21) | copy-start | bytes 18436
  16.2 452.5 %all-gather.13.cloned.1.call-start = ((), (), s32[]{:S(2)}) async-start(), calls=%async_computation.7 | async-start | bytes 2359296 | tf_op jit(solution)/shard_map/all_gather | solution.py:118
  16.9 451.8 %all-gather.19.cloned.1.call-start = ((), (), s32[]{:S(2)}) async-start(), calls=%async_computation.10 | async-start | bytes 11796480 | tf_op jit(solution)/shard_map/all_gather | solution.py:165
  17.5 1167.5 %all-gather.15.cloned.1.call-start = ((), (), s32[]{:S(2)}) async-start(), calls=%async_computation.8 | async-start | bytes 9437184 | tf_op jit(solution)/shard_map/all_gather | solution.py:119
  18.1 1193.4 %all-gather.17.cloned.1.call-start = ((), (), s32[]{:S(2)}) async-start(), calls=%async_computation.9 | async-start | bytes 9437184 | tf_op jit(solution)/shard_map/all_gather | solution.py:120
  18.7 1449.3 %all-reduce.3.cloned.1.call-start = ((), (), s32[]{:S(2)}) async-start(), calls=%async_computation.11 | async-start | bytes 18874368 | tf_op jit(solution)/shard_map/psum | solution.py:243
  21.2 183.4 %copy-start.7 = (f32[2304,16]{0,1:T(8,128)}, f32[2304,16]{0,1:T(8,128)S(1)}, u32[]{:S(2)}) copy-start(f32[2304,16]{0,1:T(8,128)S(1)} %get-tuple-element.470) | copy-start | bytes 442372
  21.2 183.4 %copy-start.9 = (f32[2304,16]{0,1:T(8,128)}, f32[2304,16]{0,1:T(8,128)S(1)}, u32[]{:S(2)}) copy-start(f32[2304,16]{0,1:T(8,128)S(1)} %get-tuple-element.471) | copy-start | bytes 442372
  1136.6 12.4 copy-start.8
  1185.0 26.4 %copy-start.25 = (f32[2048]{0:T(1024)S(1)}, f32[2048]{0:T(1024)}, u32[]{:S(2)}) copy-start(f32[2048]{0:T(1024)} %param.24) | copy-start | bytes 24580
  1279.2 837.8 %all-gather.21.cloned.1.call-start = ((), (), s32[]{:S(2)}) async-start(), calls=%async_computation.16 | async-start | bytes 94371840 | tf_op jit(solution)/shard_map/all_gather | solution.py:156
  1326.8 862.0 %reduce-scatter.10.cloned.1.call-start = ((), (), s32[]{:S(2)}) async-start(), calls=%async_computation.13 | async-start | bytes 2359296 | tf_op jit(solution)/shard_map/reduce_scatter | solution.py:232
  1336.3 890.5 %reduce-scatter.8.cloned.1.call-start = ((), (), s32[]{:S(2)}) async-start(), calls=%async_computation.12 | async-start | bytes 7077888 | tf_op jit(solution)/shard_map/reduce_scatter | solution.py:229
  1358.0 959.1 %reduce-scatter.12.cloned.1.call-start = ((), (), s32[]{:S(2)}) async-start(), calls=%async_computation.14 | async-start | bytes 9437184 | tf_op jit(solution)/shard_map/reduce_scatter | solution.py:235
  1384.7 1022.5 %reduce-scatter.14.cloned.1.call-start = ((), (), s32[]{:S(2)}) async-start(), calls=%async_computation.15 | async-start | bytes 9437184 | tf_op jit(solution)/shard_map/reduce_scatter | solution.py:238
  1415.9 52.1 %copy-start.2 = (bf16[576,2048]{1,0:T(8,128)(2,1)S(1)}, bf16[576,2048]{1,0:T(8,128)(2,1)}, u32[]{:S(2)}) copy-start(bf16[576,2048]{1,0:T(8,128)(2,1)} %param.16) | copy-start | bytes 7077892
  1415.9 52.1 %copy-start.12 = (f32[576]{0:T(1024)S(1)}, f32[576]{0:T(1024)}, u32[]{:S(2)}) copy-start(f32[576]{0:T(1024)} %copy-done.11) | copy-start | bytes 6916
  1415.9 52.1 %copy-start.14 = (f32[2048]{0:T(1024)S(1)}, f32[2048]{0:T(1024)}, u32[]{:S(2)}) copy-start(f32[2048]{0:T(1024)} %param.18) | copy-start | bytes 24580
  1415.9 1126.7 %reduce-scatter.16.cloned.1.call-start = ((), (), s32[]{:S(2)}) async-start(), calls=%async_computation.17 | async-start | bytes 1081344
  1433.4 37.3 %copy-start.18 = (f32[576]{0:T(1024)S(1)}, f32[576]{0:T(1024)}, u32[]{:S(2)}) copy-start(f32[576]{0:T(1024)} %copy-done.17) | copy-start | bytes 6916
  1433.4 37.3 %copy-start.16 = (f32[576]{0:T(1024)S(1)}, f32[576]{0:T(1024)}, u32[]{:S(2)}) copy-start(f32[576]{0:T(1024)} %copy-done.15) | copy-start | bytes 6916
  2117.0 31.3 %copy-start.19 = (f32[2048]{0:T(1024)S(1)}, f32[2048]{0:T(1024)}, u32[]{:S(2)}) copy-start(f32[2048]{0:T(1024)} %param.26) | copy-start | bytes 24580
  (16 other events, 76.1 us)
Sparse Core Ops, SparseCore 0:
  10.2 67.8 all-gather.10
  80.0 94.5 all-gather.8
  176.2 30.8 all-gather.12
  208.7 95.3 all-gather.18
  305.6 82.0 all-gather.14
  389.1 81.0 all-gather.16
  1279.3 188.6 all-reduce.2
  1469.9 647.0 all-gather.20
  2119.9 35.7 reduce-scatter.9
  2157.8 68.9 reduce-scatter.7
  2229.1 87.8 reduce-scatter.11
  2319.2 87.9 reduce-scatter.13
  2409.4 133.1 reduce-scatter.15
